TPU v7x, 128 devices: a whole 4x4x4 slice. The times are simulated.
128 devices in a mesh: gx: 8 (over y, core), gy: 4 (over z), gz: 4 (over x).
Axes of the slice: x: 4, y: 4, z: 4, core: 2. Of those that a mesh axis runs over, the one named last changes fastest.
Arguments:
- right_side: float32 [128, 64, 1024], P('gx', 'gy', 'gz'), may hold values from -8 to 8
- conductance: float32 [3, 128, 64, 1024], P(None, 'gx', 'gy', 'gz'), may hold values from 0.2 to 5
- storage: float32 [128, 64, 1024], P('gx', 'gy', 'gz'), may hold values from 0.05 to 0.8
- dirichlet: int32 [128, 64, 1024], P('gx', 'gy', 'gz'), may hold values 0 or 1
- basis: float32 [16, 128, 64, 1024], P(None, 'gx', 'gy', 'gz'), may hold values from -2 to 2
- coarse_inverse: float32 [2048, 2048], P(('gx', 'gy', 'gz')), may hold values from 0 to 2, as said below
Outputs:
- solution_field: float32 [128, 64, 1024], P('gx', 'gy', 'gz')
- residual: float32 [128, 64, 1024], P('gx', 'gy', 'gz')
Inputs may be any that keep to these rules, and one draw needn't show every extreme that they name: `coarse_inverse`: symmetric positive definite.
All inputs are finite; a program needn't handle non-finite values. No bound on the sum of `dirichlet` on one device may be relied on, other than what follows from the above.
Results may differ from a plain program's by a relative error of at most 0.0003.
Values sent between devices are 32-bit elements; how exact they have to be, the bound alone decides.
A program may use at most 128 MiB of HBM per device.

v0:
```python
import functools

import jax
import jax.numpy as jnp
from jax import lax
from jax.experimental import pallas as pl
from jax.experimental.pallas import tpu as pltpu
from jax.sharding import PartitionSpec as P

MESH_ID = pl.DeviceIdType.MESH

SWEEPS = 4
ITERS = 2


RELAX = 2.0 / 3.0


def padded(value, sides, width):
    for axis, dim in sides:
        count, length = (lax.axis_size(axis), value.shape[dim])
        up = [(i, (i + 1) % count) for i in range(count - 1)]
        down = [(j, i) for i, j in up]
        last = lax.slice_in_dim(value, length - width, length, axis=dim)
        leading = lax.slice_in_dim(value, 0, width, axis=dim)
        before = lax.ppermute(last, axis, up)
        after = lax.ppermute(leading, axis, down)
        value = jnp.concatenate([before, value, after], axis=dim)
    return value


def pad_cond(cond):
    return jnp.pad(cond, ((0, 0), (1, 1), (1, 1), (1, 1)))


def stencil(padded_free, padded_cond, field, storage, free):
    middle = padded_free[1:-1, 1:-1, 1:-1]
    total = storage * middle
    total = (
        total
        + padded_cond[0, 1:-1, 1:-1, 1:-1] * (middle - padded_free[2:, 1:-1, 1:-1])
        + padded_cond[0, :-2, 1:-1, 1:-1] * (middle - padded_free[:-2, 1:-1, 1:-1])
    )
    total = (
        total
        + padded_cond[1, 1:-1, 1:-1, 1:-1] * (middle - padded_free[1:-1, 2:, 1:-1])
        + padded_cond[1, 1:-1, :-2, 1:-1] * (middle - padded_free[1:-1, :-2, 1:-1])
    )
    total = (
        total
        + padded_cond[2, 1:-1, 1:-1, 1:-1] * (middle - padded_free[1:-1, 1:-1, 2:])
        + padded_cond[2, 1:-1, 1:-1, :-2] * (middle - padded_free[1:-1, 1:-1, :-2])
    )
    return free * total + (1.0 - free) * field


def diagonal_of(padded_cond, storage, free):
    total = storage + padded_cond[0, 1:-1, 1:-1, 1:-1] + padded_cond[0, :-2, 1:-1, 1:-1]
    total = total + padded_cond[1, 1:-1, 1:-1, 1:-1] + padded_cond[1, 1:-1, :-2, 1:-1]
    total = total + padded_cond[2, 1:-1, 1:-1, 1:-1] + padded_cond[2, 1:-1, 1:-1, :-2]
    return free * total + (1.0 - free)


def jacobi(rhs_box, padded_cond, diagonal, storage_box, free_box):
    guess = jnp.zeros_like(rhs_box)
    for sweep in range(SWEEPS):
        image = stencil(jnp.pad(free_box * guess, 1), padded_cond, guess, storage_box, free_box)
        guess = guess + RELAX * (rhs_box - image) / diagonal
    return guess


def project(basis, field):
    return jnp.sum(basis * field[None], axis=(1, 2, 3))


def expand(basis, weights, field):
    return jnp.sum(weights[:, None, None, None] * basis, axis=0)


LANES = 128


def residual_rim(field):
    return padded(field, (("gx", 0), ("gy", 1), ("gz", 2)), 2)


def gather_kernel(sizes, row_ref, out_ref, held, local_sem, send1, recv1, send2, recv2, send3, recv3):
    nx, ny, nz = sizes
    a = lax.axis_index("gx")
    b = lax.axis_index("gy")
    c = lax.axis_index("gz")
    me = (a * ny + b) * nz + c

    def along_z(k):
        return (a, b, lax.rem(c + k, nz))

    def along_y(k):
        return (a, lax.rem(b + k, ny), c)

    def along_x(k):
        return (lax.rem(a + k, nx), b, c)

    peers = [along_z(k) for k in range(1, nz)]
    peers += [along_y(k) for k in range(1, ny)]
    peers += [along_x(k) for k in range(1, nx)]
    barrier = pltpu.get_barrier_semaphore()
    for peer in peers:
        pl.semaphore_signal(barrier, inc=1, device_id=peer, device_id_type=MESH_ID)
    pl.semaphore_wait(barrier, len(peers))

    own = pltpu.make_async_copy(row_ref, held.at[pl.ds(me, 1)], local_sem.at[0])
    own.start()
    sent = []

    def stage(src_of, first_of, count, size, toward, send, recv):
        for k in range(1, size):
            copy = pltpu.make_async_remote_copy(
                src_ref=src_of(0),
                dst_ref=held.at[pl.ds(first_of(0), count)],
                send_sem=send.at[k],
                recv_sem=recv.at[k],
                device_id=toward(k),
                device_id_type=MESH_ID,
            )
            copy.start()
            sent.append(copy)
        for k in range(1, size):
            pltpu.make_async_remote_copy(
                src_ref=src_of(k),
                dst_ref=held.at[pl.ds(first_of(k), count)],
                send_sem=send.at[k],
                recv_sem=recv.at[k],
                device_id=toward(size - k),
                device_id_type=MESH_ID,
            ).wait_recv()

    z_first = lambda k: (a * ny + b) * nz + lax.rem(c + nz - k, nz)
    stage(lambda k: row_ref, z_first, 1, nz, along_z, send1, recv1)
    own.wait()
    y_first = lambda k: (a * ny + lax.rem(b + ny - k, ny)) * nz
    stage(lambda k: held.at[pl.ds(y_first(k), nz)], y_first, nz, ny, along_y, send2, recv2)
    x_first = lambda k: lax.rem(a + nx - k, nx) * ny * nz
    stage(lambda k: held.at[pl.ds(x_first(k), ny * nz)], x_first, ny * nz, nx, along_x, send3, recv3)
    for copy in sent:
        copy.wait_send()
    final = pltpu.make_async_copy(held, out_ref, local_sem.at[1])
    final.start()
    final.wait()


def gather_rows(row):
    sizes = (lax.axis_size("gx"), lax.axis_size("gy"), lax.axis_size("gz"))
    count = sizes[0] * sizes[1] * sizes[2]
    tile = row[:, None, :]
    rows = pl.pallas_call(
        functools.partial(gather_kernel, sizes),
        out_shape=jax.ShapeDtypeStruct((count, 1, LANES), jnp.float32),
        in_specs=[pl.BlockSpec(memory_space=pltpu.VMEM)],
        out_specs=pl.BlockSpec(memory_space=pltpu.VMEM),
        scratch_shapes=[
            pltpu.VMEM((count, 1, LANES), jnp.float32),
            pltpu.SemaphoreType.DMA((2,)),
            pltpu.SemaphoreType.DMA((sizes[2],)),
            pltpu.SemaphoreType.DMA((sizes[2],)),
            pltpu.SemaphoreType.DMA((sizes[1],)),
            pltpu.SemaphoreType.DMA((sizes[1],)),
            pltpu.SemaphoreType.DMA((sizes[0],)),
            pltpu.SemaphoreType.DMA((sizes[0],)),
        ],
        compiler_params=pltpu.CompilerParams(collective_id=0, has_side_effects=True),
    )(tile)
    return rows[:, 0, :]


def pack(coarse, scalars):
    vecs = coarse.shape[0]
    row = jnp.zeros((LANES,), jnp.float32)
    row = row.at[:vecs].set(coarse)
    if scalars:
        row = row.at[vecs:vecs + len(scalars)].set(jnp.stack(scalars))
    return row[None]


def unpack(rows, vecs, count):
    coarse = rows[:, :vecs].reshape(-1)
    sums = jnp.sum(rows[:, vecs:vecs + count], axis=0)
    return coarse, [sums[i] for i in range(count)]


def shards(right_side, conductance, storage, dirichlet, basis, coarse_inverse):
    vecs = basis.shape[0]
    sides = (("gx", 0), ("gy", 1), ("gz", 2))
    free = 1.0 - dirichlet.astype(jnp.float32)
    stacked = jnp.concatenate([conductance, storage[None], free[None], right_side[None]], axis=0)
    wide = padded(stacked, (("gx", 1), ("gy", 2), ("gz", 3)), 3)
    cond_wide = wide[:3]
    free_wide = wide[4]
    storage_wide = wide[3]
    cond_box = wide[:3, 1:-1, 1:-1, 1:-1]
    storage_box = wide[3, 1:-1, 1:-1, 1:-1]
    free_box = wide[4, 1:-1, 1:-1, 1:-1]
    rhs_box0 = wide[5, 1:-1, 1:-1, 1:-1]
    box_cond = pad_cond(cond_box)
    box_diag = diagonal_of(box_cond, storage_box, free_box)
    cond_face = wide[:3, 2:-2, 2:-2, 2:-2]
    free_face = wide[4, 2:-2, 2:-2, 2:-2]

    def schwarz(rhs_box):
        return jacobi(rhs_box, box_cond, box_diag, storage_box, free_box)[2:-2, 2:-2, 2:-2]

    def precondition(rhs_box, residual, coarse_all):
        weights = jnp.dot(coarse_inverse, coarse_all, precision=lax.Precision.HIGHEST)
        return schwarz(rhs_box) + expand(basis, weights, residual)

    residual0 = right_side
    coarse0 = project(basis, residual0)
    coarse0_all, _ = unpack(gather_rows(pack(coarse0, [])), vecs, 0)
    z0 = precondition(rhs_box0, residual0, coarse0_all)
    near0 = padded(z0, sides, 3)
    inner = (slice(1, -1),) * 3
    image0_box = stencil(free_wide * near0, cond_wide, near0[inner], storage_wide[inner], free_wide[inner])
    image0 = image0_box[2:-2, 2:-2, 2:-2]
    coarse_img = project(basis, image0)
    rows = gather_rows(pack(coarse_img, [jnp.sum(residual0 * z0), jnp.sum(z0 * image0)]))
    coarse_img_all, (rz0, curve0) = unpack(rows, vecs, 2)
    alpha0 = rz0 / curve0
    solution1 = alpha0 * z0
    rhs_box1 = rhs_box0 - alpha0 * image0_box
    residual1 = rhs_box1[2:-2, 2:-2, 2:-2]
    coarse1_all = coarse0_all - alpha0 * coarse_img_all
    z1 = precondition(rhs_box1, residual1, coarse1_all)
    near1 = padded(z1, sides, 1)
    image_z1 = stencil(free_face * near1, cond_face, z1, storage, free)
    local = [
        jnp.sum(residual1 * z1),
        jnp.sum(z1 * image_z1),
        jnp.sum(z1 * image0),
        jnp.sum(z0 * image_z1),
    ]
    _, (rz1, zz, cross_a, cross_b) = unpack(gather_rows(pack(jnp.zeros((0,), jnp.float32), local)), 0, 4)
    beta = rz1 / rz0
    direction1 = z1 + beta * z0
    image1 = image_z1 + beta * image0
    curve1 = zz + beta * (cross_a + cross_b) + beta * beta * curve0
    alpha1 = rz1 / curve1
    solution2 = solution1 + alpha1 * direction1
    residual2 = residual1 - alpha1 * image1
    return (solution2, residual2)


def solution(mesh):
    placed = (
        P("gx", "gy", "gz"),
        P(None, "gx", "gy", "gz"),
        P("gx", "gy", "gz"),
        P("gx", "gy", "gz"),
        P(None, "gx", "gy", "gz"),
        P(("gx", "gy", "gz"), None),
    )
    return jax.shard_map(
        shards,
        mesh=mesh,
        in_specs=placed,
        out_specs=(P("gx", "gy", "gz"), P("gx", "gy", "gz")),
        check_vma=False,
    )
```

profile of v0, /device:TPU:1, one launch (start us, length us, event | category | flops | bytes accessed | tf_op | source)
XLA Modules:
  0.0 215.4 jit_solution(242438933431629001)
XLA Ops:
  3.3 3.3 %collective-permute-start.1 = (f32[6,3,16,256]{3,2,1,0:T(8,128)S(1)}, f32[6,3,16,256]{3,2,1,0:T(8,128)S(1)}, u32[]{:S(2)}, u32[]{:S(2)}) collective-permute-start(f32[6,3,16,256]{3,2,1,0:T(8,128)S(1)} %get-tuple-element.84), channel_id=1, source_target_pairs={{16,0},{32,16},{48,32},{64,48},{80,64},{96,80},{112,96},{17,1},{33... | collective-permute-start | bytes 884744 | tf_op jit(solution)/shard_map/ppermute | solution.py:27
  6.6 3.2 %collective-permute-start = (f32[6,3,16,256]{3,2,1,0:T(8,128)S(1)}, f32[6,3,16,256]{3,2,1,0:T(8,128)S(1)}, u32[]{:S(2)}, u32[]{:S(2)}) collective-permute-start(f32[6,3,16,256]{3,2,1,0:T(8,128)S(1)} %get-tuple-element.83), channel_id=1, source_target_pairs={{0,16},{16,32},{32,48},{48,64},{64,80},{80,96},{96,112},{1,17},{17... | collective-permute-start | bytes 884744 | tf_op jit(solution)/shard_map/ppermute | solution.py:26
  9.8 2.5 %collective-permute-done.1 = f32[6,3,16,256]{3,2,1,0:T(8,128)S(1)} collective-permute-done((f32[6,3,16,256]{3,2,1,0:T(8,128)S(1)}, f32[6,3,16,256]{3,2,1,0:T(8,128)S(1)}, u32[]{:S(2)}, u32[]{:S(2)}) %collective-permute-start.1) | collective-permute-done | bytes 294944 | tf_op jit(solution)/shard_map/ppermute | solution.py:27
  17.5 4.9 %collective-permute-start.2 = (f32[6,22,3,256]{3,1,2,0:T(8,128)}, f32[6,22,3,256]{3,1,2,0:T(8,128)}, u32[]{:S(2)}, u32[]{:S(2)}) collective-permute-start(f32[6,22,3,256]{3,1,2,0:T(8,128)} %copy.25), channel_id=1, source_target_pairs={{0,4},{4,8},{8,12},{1,5},{5,9},{9,13},{2,6},{6,10},{10,14},{3,7},{... | collective-permute-start | bytes 1216520 | tf_op jit(solution)/shard_map/ppermute | solution.py:26
  23.6 18.7 %shard_map.77 = f32[128,1,128]{2,1,0:T(1,128)} custom-call(f32[1,1,128]{2,1,0:T(1,128)} %scatter.14.row_ref), custom_call_target="tpu_custom_call" | custom-call | tf_op jit(solution)/shard_map/pallas_call | solution.py:155
  48.5 2.4 %copy.30 = f32[6,22,22,3]{2,1,3,0:T(8,128)S(1)} copy(f32[6,22,22,3]{3,2,1,0:T(8,128)} %get-tuple-element.80) | data formatting | bytes 69696 | tf_op jit(solution)/shard_map/slice | solution.py:25
  53.9 4.7 %collective-permute-start.4 = (f32[6,22,22,3]{2,1,3,0:T(8,128)}, f32[6,22,22,3]{2,1,3,0:T(8,128)}, u32[]{:S(2)}, u32[]{:S(2)}) collective-permute-start(f32[6,22,22,3]{2,1,3,0:T(8,128)} %copy.29), channel_id=1, source_target_pairs={{0,1},{1,2},{2,3},{4,5},{5,6},{6,7},{8,9},{9,10},{10,11},{12,13},{... | collective-permute-start | bytes 104552 | tf_op jit(solution)/shard_map/ppermute | solution.py:26
  58.5 3.5 %multiply_reduce_fusion.2 = f32[16,16,256]{2,1,0:T(8,128)} fusion(f32[16,16,16,256]{3,2,1,0:T(8,128)} %param.18, f32[16]{0:T(128)S(1)} %convolution_bitcast_fusion.1), kind=kLoop, calls=%fused_computation.4 | loop fusion | flops 2031616 | bytes 4456512 | tf_op jit(solution)/shard_map/reduce_sum | solution.py:77
  62.0 3.0 %copy.32 = f32[6,22,22,3]{3,2,1,0:T(8,128)} copy(f32[6,22,22,3]{2,1,3,0:T(8,128)} %collective-permute-done.5) | data formatting | bytes 69696 | tf_op jit(solution)/shard_map/ppermute | solution.py:27
  65.0 1.9 copy.31
  66.9 9.6 %pad_maximum_fusion = f32[6,22,22,262]{3,2,1,0:T(8,128)S(1)} fusion(f32[6,22,22,3]{3,2,1,0:T(8,128)} %copy.32, f32[6,22,3,256]{3,2,1,0:T(4,128)} %copy-done.20, f32[6,3,16,256]{3,2,1,0:T(8,128)} %copy-done.26, f32[1,16,16,256]{3,2,1,0:T(8,128)S(1)} %bitcast.309, f32[1,16,16,256]{3,2,1,0:T(8,128)S(1)} %fusion.198, f32[1,16,16,256]{3,2,1,0:T(8,128)S(1)} %bitcast.314, ...), kind=kLoop, calls=%fused_computation | loop fusion | flops 6847632 | bytes 6086784 | tf_op jit(solution)/shard_map/concatenate | solution.py:28
  78.2 2.4 %fusion.199 = (f32[20,20,260]{2,1,0:T(8,128)S(1)}, f32[20,20,260]{2,1,0:T(8,128)S(1)}, f32[20,20,260]{2,1,0:T(8,128)S(1)}, f32[20,20,260]{2,1,0:T(8,128)S(1)}) fusion(f32[6,22,22,262]{3,2,1,0:T(8,128)S(1)} %pad_maximum_fusion, f32[20,20,260]{2,1,0:T(8,128)S(1)} %broadcast_multiply_fusion, f32[3,20,20,260]{3,2,1,0:T(8,128)S(1)} %slice.610), kind=kLoop, calls=%fused_computation.326 | loop fusion | flops 3640000 | bytes 5824000 | tf_op jit(solution)/shard_map/mul | solution.py:67
  80.6 2.3 %fusion.205 = (f32[20,20,260]{2,1,0:T(8,128)S(1)}, f32[20,20,260]{2,1,0:T(8,128)S(1)}) fusion(f32[6,22,22,262]{3,2,1,0:T(8,128)S(1)} %pad_maximum_fusion, f32[20,20,260]{2,1,0:T(8,128)S(1)} %get-tuple-element.73, f32[20,20,260]{2,1,0:T(8,128)S(1)} %get-tuple-element.71, f32[3,20,20,260]{3,2,1,0:T(8,128)S(1)} %slice.610, f32[20,20,260]{2,1,0:T(8,128)S(1)} %get-tuple-element.72), kind=kLoop, calls=%fused_computation.344 | loop fusion | flops 3224000 | bytes 5824000 | tf_op jit(solution)/shard_map/mul | solution.py:67
  82.9 2.1 fusion.204
  87.2 2.9 %collective-permute-start.7 = (f32[3,16,256]{2,1,0:T(8,128)S(1)}, f32[3,16,256]{2,1,0:T(8,128)S(1)}, u32[]{:S(2)}, u32[]{:S(2)}) collective-permute-start(f32[3,16,256]{2,1,0:T(8,128)S(1)} %get-tuple-element.97), channel_id=1, source_target_pairs={{16,0},{32,16},{48,32},{64,48},{80,64},{96,80},{112,96},{17,1},{33... | collective-permute-start | bytes 147464 | tf_op jit(solution)/shard_map/ppermute | solution.py:27
  90.1 2.9 %collective-permute-start.6 = (f32[3,16,256]{2,1,0:T(8,128)S(1)}, f32[3,16,256]{2,1,0:T(8,128)S(1)}, u32[]{:S(2)}, u32[]{:S(2)}) collective-permute-start(f32[3,16,256]{2,1,0:T(8,128)S(1)} %get-tuple-element.96), channel_id=1, source_target_pairs={{0,16},{16,32},{32,48},{48,64},{64,80},{80,96},{96,112},{1,17},{17... | collective-permute-start | bytes 147464 | tf_op jit(solution)/shard_map/ppermute | solution.py:26
  95.9 4.6 %collective-permute-start.8 = (f32[22,3,256]{2,1,0:T(4,128)}, f32[22,3,256]{2,1,0:T(4,128)}, u32[]{:S(2)}, u32[]{:S(2)}) collective-permute-start(f32[22,3,256]{2,1,0:T(4,128)} %get-tuple-element.90), channel_id=1, source_target_pairs={{0,4},{4,8},{8,12},{1,5},{5,9},{9,13},{2,6},{6,10},{10,14},{3,7},{... | collective-permute-start | bytes 202760 | tf_op jit(solution)/shard_map/ppermute | solution.py:26
  105.1 4.0 %collective-permute-start.10 = (f32[22,22,3]{2,1,0:T(8,128)S(1)}, f32[22,22,3]{2,1,0:T(8,128)S(1)}, u32[]{:S(2)}, u32[]{:S(2)}) collective-permute-start(f32[22,22,3]{2,1,0:T(8,128)S(1)} %get-tuple-element.86), channel_id=1, source_target_pairs={{0,1},{1,2},{2,3},{4,5},{5,6},{6,7},{8,9},{9,10},{10,11},{12,13},{... | collective-permute-start | bytes 17432 | tf_op jit(solution)/shard_map/ppermute | solution.py:26
  110.6 2.8 %collective-permute-done.11 = f32[22,22,3]{2,1,0:T(8,128)S(1)} collective-permute-done((f32[22,22,3]{2,1,0:T(8,128)S(1)}, f32[22,22,3]{2,1,0:T(8,128)S(1)}, u32[]{:S(2)}, u32[]{:S(2)}) %collective-permute-start.11) | collective-permute-done | bytes 5840 | tf_op jit(solution)/shard_map/ppermute | solution.py:27
  115.8 3.0 %fusion.155 = f32[20,20,260]{2,1,0:T(8,128)S(1)} fusion(f32[22,22,262]{2,1,0:T(8,128)S(1)} %get-tuple-element.66, f32[22,22,262]{2,1,0:T(8,128)S(1)} %get-tuple-element.65, f32[6,22,22,262]{3,2,1,0:T(8,128)S(1)} %copy-done.2, f32[22,22,262]{2,1,0:T(8,128)S(1)} %get-tuple-element.75, f32[22,22,262]{2,1,0:T(8,128)S(1)} %get-tuple-element.74), kind=kLoop, calls=%fused_computation.213 | loop fusion | flops 2392000 | bytes 7072000 | tf_op jit(solution)/shard_map/add | solution.py:54
  122.1 18.0 %shard_map.78 = f32[128,1,128]{2,1,0:T(1,128)} custom-call(f32[1,1,128]{2,1,0:T(1,128)} %copy-done.37), custom_call_target="tpu_custom_call" | custom-call | tf_op jit(solution)/shard_map/pallas_call | solution.py:155
  143.9 3.6 %fusion.200 = (f32[20,20,260]{2,1,0:T(8,128)}, f32[20,20,260]{2,1,0:T(8,128)}) fusion(f32[20,20,260]{2,1,0:T(8,128)} %copy-done.6, f32[20,20,260]{2,1,0:T(8,128)} %copy-done.18, f32[6,22,22,262]{3,2,1,0:T(8,128)} %copy-done.1, f32[20,20,260]{2,1,0:T(8,128)} %copy-done.24, f32[]{:T(128)S(6)} %div.37), kind=kLoop, calls=%fused_computation.327 | loop fusion | flops 624000 | bytes 2912004 | tf_op jit(solution)/shard_map/mul | solution.py:67
  147.8 3.0 %multiply_reduce_fusion = f32[16,16,256]{2,1,0:T(8,128)S(1)} fusion(f32[16,16,16,256]{3,2,1,0:T(8,128)} %param.18, f32[16]{0:T(128)S(1)} %convolution_bitcast_fusion), kind=kLoop, calls=%fused_computation.2 | loop fusion | flops 2031616 | bytes 4456512 | tf_op jit(solution)/shard_map/reduce_sum | solution.py:77
  150.9 4.0 %fusion.203 = (f32[20,20,260]{2,1,0:T(8,128)S(1)}, f32[20,20,260]{2,1,0:T(8,128)S(1)}) fusion(f32[6,22,22,262]{3,2,1,0:T(8,128)} %copy-done.1, f32[20,20,260]{2,1,0:T(8,128)S(1)} %copy-done.7, f32[20,20,260]{2,1,0:T(8,128)S(1)} %copy-done.17, f32[20,20,260]{2,1,0:T(8,128)S(1)} %copy-done.30, f32[3,20,20,260]{3,2,1,0:T(8,128)S(1)} %slice.610, ...), kind=kLoop, calls=%fused_computation.342 | loop fusion | flops 3224000 | bytes 5824000 | tf_op jit(solution)/shard_map/mul | solution.py:67
  160.2 2.3 %collective-permute-start.13 = (f32[1,16,256]{2,1,0:T(8,128)S(1)}, f32[1,16,256]{2,1,0:T(8,128)S(1)}, u32[]{:S(2)}, u32[]{:S(2)}) collective-permute-start(f32[1,16,256]{2,1,0:T(8,128)S(1)} %get-tuple-element.95), channel_id=1, source_target_pairs={{16,0},{32,16},{48,32},{64,48},{80,64},{96,80},{112,96},{17,1},{33... | collective-permute-start | bytes 49160 | tf_op jit(solution)/shard_map/ppermute | solution.py:27
  162.5 3.3 %collective-permute-start.12 = (f32[1,16,256]{2,1,0:T(8,128)S(1)}, f32[1,16,256]{2,1,0:T(8,128)S(1)}, u32[]{:S(2)}, u32[]{:S(2)}) collective-permute-start(f32[1,16,256]{2,1,0:T(8,128)S(1)} %get-tuple-element.94), channel_id=1, source_target_pairs={{0,16},{16,32},{32,48},{48,64},{64,80},{80,96},{96,112},{1,17},{17... | collective-permute-start | bytes 49160 | tf_op jit(solution)/shard_map/ppermute | solution.py:26
  168.0 4.0 %collective-permute-start.14 = (f32[18,1,256]{2,1,0:T(1,128)S(1)}, f32[18,1,256]{2,1,0:T(1,128)S(1)}, u32[]{:S(2)}, u32[]{:S(2)}) collective-permute-start(f32[18,1,256]{2,1,0:T(1,128)S(1)} %get-tuple-element.92), channel_id=1, source_target_pairs={{0,4},{4,8},{8,12},{1,5},{5,9},{9,13},{2,6},{6,10},{10,14},{3,7},{... | collective-permute-start | bytes 55304 | tf_op jit(solution)/shard_map/ppermute | solution.py:26
  174.7 4.0 %collective-permute-start.16 = (f32[18,18,1]{2,1,0:T(8,128)S(1)}, f32[18,18,1]{2,1,0:T(8,128)S(1)}, u32[]{:S(2)}, u32[]{:S(2)}) collective-permute-start(f32[18,18,1]{2,1,0:T(8,128)S(1)} %get-tuple-element.88), channel_id=1, source_target_pairs={{0,1},{1,2},{2,3},{4,5},{5,6},{6,7},{8,9},{9,10},{10,11},{12,13},{... | collective-permute-start | bytes 3896 | tf_op jit(solution)/shard_map/ppermute | solution.py:26
  179.6 2.5 %collective-permute-done.17 = f32[18,18,1]{2,1,0:T(8,128)S(1)} collective-permute-done((f32[18,18,1]{2,1,0:T(8,128)S(1)}, f32[18,18,1]{2,1,0:T(8,128)S(1)}, u32[]{:S(2)}, u32[]{:S(2)}) %collective-permute-start.17) | collective-permute-done | bytes 1328 | tf_op jit(solution)/shard_map/ppermute | solution.py:27
  185.2 2.7 %maximum_bitcast_fusion.1 = f32[1,1,4]{2,1,0:T(1,128)S(1)} fusion(f32[1]{0:T(128)} %bitcast.39, f32[1]{0:T(128)} %bitcast.38, f32[1]{0:T(128)} %bitcast.37, f32[1]{0:T(128)} %bitcast.29), kind=kLoop, calls=%fused_computation.338 | loop fusion | flops 12 | bytes 32 | tf_op jit(solution)/shard_map/broadcast_in_dim;broadcast_in_dim | solution.py:154
  188.4 18.9 %shard_map.79 = f32[128,1,128]{2,1,0:T(1,128)} custom-call(f32[1,1,128]{2,1,0:T(1,128)} %scatter.19.row_ref), custom_call_target="tpu_custom_call" | custom-call | tf_op jit(solution)/shard_map/pallas_call | solution.py:155
  213.4 2.1 multiply_subtract_fusion.1
  (152 shorter events, 55.2 us)
Async XLA Ops:
  0.6 42.6 %copy-start = (f32[16,2048]{1,0:T(8,128)S(1)}, f32[16,2048]{1,0:T(8,128)}, u32[]{:S(2)}) copy-start(f32[16,2048]{1,0:T(8,128)} %param.19) | copy-start | bytes 393220
  0.6 21.8 %copy-start.10 = (f32[16,16,256]{2,1,0:T(8,128)S(1)}, f32[16,16,256]{2,1,0:T(8,128)}, u32[]{:S(2)}) copy-start(f32[16,16,256]{2,1,0:T(8,128)} %param.14) | copy-start | bytes 786436
  0.7 21.8 %copy-start.3 = (f32[16,16,16,256]{3,2,1,0:T(8,128)S(1)}, f32[16,16,16,256]{3,2,1,0:T(8,128)}, u32[]{:S(2)}) copy-start(f32[16,16,16,256]{3,2,1,0:T(8,128)} %param.18) | copy-start | bytes 12582916
  1.8 65.1 %copy-start.13 = (f32[1,16,16,256]{3,2,1,0:T(8,128)}, f32[1,16,16,256]{3,2,1,0:T(8,128)S(1)}, u32[]{:S(2)}) copy-start(f32[1,16,16,256]{3,2,1,0:T(8,128)S(1)} %fusion.198) | copy-start | bytes 786436
  3.3 9.0 %collective-permute-start.1 = (f32[6,3,16,256]{3,2,1,0:T(8,128)S(1)}, f32[6,3,16,256]{3,2,1,0:T(8,128)S(1)}, u32[]{:S(2)}, u32[]{:S(2)}) collective-permute-start(f32[6,3,16,256]{3,2,1,0:T(8,128)S(1)} %get-tuple-element.84), channel_id=1, source_target_pairs={{16,0},{32,16},{48,32},{64,48},{80,64},{96,80},{112,96},{17,1},{33... | collective-permute-start | bytes 884744 | tf_op jit(solution)/shard_map/ppermute | solution.py:27
  6.6 6.8 %collective-permute-start = (f32[6,3,16,256]{3,2,1,0:T(8,128)S(1)}, f32[6,3,16,256]{3,2,1,0:T(8,128)S(1)}, u32[]{:S(2)}, u32[]{:S(2)}) collective-permute-start(f32[6,3,16,256]{3,2,1,0:T(8,128)S(1)} %get-tuple-element.83), channel_id=1, source_target_pairs={{0,16},{16,32},{32,48},{48,64},{64,80},{80,96},{96,112},{1,17},{17... | collective-permute-start | bytes 884744 | tf_op jit(solution)/shard_map/ppermute | solution.py:26
  12.3 32.8 %copy-start.26 = (f32[6,3,16,256]{3,2,1,0:T(8,128)}, f32[6,3,16,256]{3,2,1,0:T(8,128)S(1)}, u32[]{:S(2)}) copy-start(f32[6,3,16,256]{3,2,1,0:T(8,128)S(1)} %collective-permute-done.1) | copy-start | bytes 884740
  13.5 31.6 %copy-start.28 = (f32[6,3,16,256]{3,2,1,0:T(8,128)}, f32[6,3,16,256]{3,2,1,0:T(8,128)S(1)}, u32[]{:S(2)}) copy-start(f32[6,3,16,256]{3,2,1,0:T(8,128)S(1)} %collective-permute-done) | copy-start | bytes 884740
  15.2 30.8 %copy-start.5 = (f32[3,16,16,256]{3,2,1,0:T(8,128)S(1)}, f32[3,16,16,256]{3,2,1,0:T(8,128)}, u32[]{:S(2)}) copy-start(f32[3,16,16,256]{3,2,1,0:T(8,128)} %param.15) | copy-start | bytes 2359300
  15.2 30.8 %copy-start.15 = (f32[16,16,256]{2,1,0:T(8,128)S(1)}, f32[16,16,256]{2,1,0:T(8,128)}, u32[]{:S(2)}) copy-start(f32[16,16,256]{2,1,0:T(8,128)} %param.16) | copy-start | bytes 786436
  15.3 28.1 %collective-permute-start.3 = (f32[6,22,3,256]{3,1,2,0:T(8,128)S(1)}, f32[6,22,3,256]{3,1,2,0:T(8,128)S(1)}, u32[]{:S(2)}, u32[]{:S(2)}) collective-permute-start(f32[6,22,3,256]{3,1,2,0:T(8,128)S(1)} %copy.26), channel_id=1, source_target_pairs={{4,0},{8,4},{12,8},{5,1},{9,5},{13,9},{6,2},{10,6},{14,10},{7,3},{... | collective-permute-start | bytes 1216520 | tf_op jit(solution)/shard_map/ppermute | solution.py:27
  17.5 26.1 %collective-permute-start.2 = (f32[6,22,3,256]{3,1,2,0:T(8,128)}, f32[6,22,3,256]{3,1,2,0:T(8,128)}, u32[]{:S(2)}, u32[]{:S(2)}) collective-permute-start(f32[6,22,3,256]{3,1,2,0:T(8,128)} %copy.25), channel_id=1, source_target_pairs={{0,4},{4,8},{8,12},{1,5},{5,9},{9,13},{2,6},{6,10},{10,14},{3,7},{... | collective-permute-start | bytes 1216520 | tf_op jit(solution)/shard_map/ppermute | solution.py:26
  50.9 11.1 %collective-permute-start.5 = (f32[6,22,22,3]{2,1,3,0:T(8,128)S(1)}, f32[6,22,22,3]{2,1,3,0:T(8,128)}, u32[]{:S(2)}, u32[]{:S(2)}) collective-permute-start(f32[6,22,22,3]{2,1,3,0:T(8,128)S(1)} %copy.30), channel_id=1, source_target_pairs={{1,0},{2,1},{3,2},{5,4},{6,5},{7,6},{9,8},{10,9},{11,10},{13,12},{... | collective-permute-start | bytes 104552 | tf_op jit(solution)/shard_map/ppermute | solution.py:27
  53.9 11.2 %collective-permute-start.4 = (f32[6,22,22,3]{2,1,3,0:T(8,128)}, f32[6,22,22,3]{2,1,3,0:T(8,128)}, u32[]{:S(2)}, u32[]{:S(2)}) collective-permute-start(f32[6,22,22,3]{2,1,3,0:T(8,128)} %copy.29), channel_id=1, source_target_pairs={{0,1},{1,2},{2,3},{4,5},{5,6},{6,7},{8,9},{9,10},{10,11},{12,13},{... | collective-permute-start | bytes 104552 | tf_op jit(solution)/shard_map/ppermute | solution.py:26
  85.0 15.5 %copy-start.35 = (f32[128,1,128]{2,1,0:T(1,128)S(1)}, f32[128,1,128]{2,1,0:T(1,128)}, u32[]{:S(2)}) copy-start(f32[128,1,128]{2,1,0:T(1,128)} %shard_map.77) | copy-start | bytes 196612
  87.2 5.8 %collective-permute-start.7 = (f32[3,16,256]{2,1,0:T(8,128)S(1)}, f32[3,16,256]{2,1,0:T(8,128)S(1)}, u32[]{:S(2)}, u32[]{:S(2)}) collective-permute-start(f32[3,16,256]{2,1,0:T(8,128)S(1)} %get-tuple-element.97), channel_id=1, source_target_pairs={{16,0},{32,16},{48,32},{64,48},{80,64},{96,80},{112,96},{17,1},{33... | collective-permute-start | bytes 147464 | tf_op jit(solution)/shard_map/ppermute | solution.py:27
  90.1 3.9 %collective-permute-start.6 = (f32[3,16,256]{2,1,0:T(8,128)S(1)}, f32[3,16,256]{2,1,0:T(8,128)S(1)}, u32[]{:S(2)}, u32[]{:S(2)}) collective-permute-start(f32[3,16,256]{2,1,0:T(8,128)S(1)} %get-tuple-element.96), channel_id=1, source_target_pairs={{0,16},{16,32},{32,48},{48,64},{64,80},{80,96},{96,112},{1,17},{17... | collective-permute-start | bytes 147464 | tf_op jit(solution)/shard_map/ppermute | solution.py:26
  94.6 6.6 %collective-permute-start.9 = (f32[22,3,256]{2,1,0:T(4,128)}, f32[22,3,256]{2,1,0:T(4,128)}, u32[]{:S(2)}, u32[]{:S(2)}) collective-permute-start(f32[22,3,256]{2,1,0:T(4,128)} %get-tuple-element.91), channel_id=1, source_target_pairs={{4,0},{8,4},{12,8},{5,1},{9,5},{13,9},{6,2},{10,6},{14,10},{7,3},{... | collective-permute-start | bytes 202760 | tf_op jit(solution)/shard_map/ppermute | solution.py:27
  95.9 6.6 %collective-permute-start.8 = (f32[22,3,256]{2,1,0:T(4,128)}, f32[22,3,256]{2,1,0:T(4,128)}, u32[]{:S(2)}, u32[]{:S(2)}) collective-permute-start(f32[22,3,256]{2,1,0:T(4,128)} %get-tuple-element.90), channel_id=1, source_target_pairs={{0,4},{4,8},{8,12},{1,5},{5,9},{9,13},{2,6},{6,10},{10,14},{3,7},{... | collective-permute-start | bytes 202760 | tf_op jit(solution)/shard_map/ppermute | solution.py:26
  101.2 13.1 %copy-start.2 = (f32[6,22,22,262]{3,2,1,0:T(8,128)S(1)}, f32[6,22,22,262]{3,2,1,0:T(8,128)}, u32[]{:S(2)}) copy-start(f32[6,22,22,262]{3,2,1,0:T(8,128)} %copy-done.1) | copy-start | bytes 9130180
  103.8 9.6 %collective-permute-start.11 = (f32[22,22,3]{2,1,0:T(8,128)S(1)}, f32[22,22,3]{2,1,0:T(8,128)S(1)}, u32[]{:S(2)}, u32[]{:S(2)}) collective-permute-start(f32[22,22,3]{2,1,0:T(8,128)S(1)} %get-tuple-element.87), channel_id=1, source_target_pairs={{1,0},{2,1},{3,2},{5,4},{6,5},{7,6},{9,8},{10,9},{11,10},{13,12},{... | collective-permute-start | bytes 17432 | tf_op jit(solution)/shard_map/ppermute | solution.py:27
  105.1 9.2 %collective-permute-start.10 = (f32[22,22,3]{2,1,0:T(8,128)S(1)}, f32[22,22,3]{2,1,0:T(8,128)S(1)}, u32[]{:S(2)}, u32[]{:S(2)}) collective-permute-start(f32[22,22,3]{2,1,0:T(8,128)S(1)} %get-tuple-element.86), channel_id=1, source_target_pairs={{0,1},{1,2},{2,3},{4,5},{5,6},{6,7},{8,9},{9,10},{10,11},{12,13},{... | collective-permute-start | bytes 17432 | tf_op jit(solution)/shard_map/ppermute | solution.py:26
  119.6 28.0 %copy-start.36 = (f32[2048]{0:T(1024)S(1)}, f32[2048]{0:T(1024)}, u32[]{:S(2)}) copy-start(f32[2048]{0:T(1024)} %reshape.101) | copy-start | bytes 24580
  156.8 21.9 %copy-start.14 = (f32[1,16,16,256]{3,2,1,0:T(8,128)S(1)}, f32[1,16,16,256]{3,2,1,0:T(8,128)}, u32[]{:S(2)}) copy-start(f32[1,16,16,256]{3,2,1,0:T(8,128)} %copy-done.13) | copy-start | bytes 786436
  156.8 21.9 %copy-start.16 = (f32[16,16,256]{2,1,0:T(8,128)S(1)}, f32[16,16,256]{2,1,0:T(8,128)}, u32[]{:S(2)}) copy-start(f32[16,16,256]{2,1,0:T(8,128)} %param.16) | copy-start | bytes 786436
  160.2 5.6 %collective-permute-start.13 = (f32[1,16,256]{2,1,0:T(8,128)S(1)}, f32[1,16,256]{2,1,0:T(8,128)S(1)}, u32[]{:S(2)}, u32[]{:S(2)}) collective-permute-start(f32[1,16,256]{2,1,0:T(8,128)S(1)} %get-tuple-element.95), channel_id=1, source_target_pairs={{16,0},{32,16},{48,32},{64,48},{80,64},{96,80},{112,96},{17,1},{33... | collective-permute-start | bytes 49160 | tf_op jit(solution)/shard_map/ppermute | solution.py:27
  162.5 4.1 %collective-permute-start.12 = (f32[1,16,256]{2,1,0:T(8,128)S(1)}, f32[1,16,256]{2,1,0:T(8,128)S(1)}, u32[]{:S(2)}, u32[]{:S(2)}) collective-permute-start(f32[1,16,256]{2,1,0:T(8,128)S(1)} %get-tuple-element.94), channel_id=1, source_target_pairs={{0,16},{16,32},{32,48},{48,64},{64,80},{80,96},{96,112},{1,17},{17... | collective-permute-start | bytes 49160 | tf_op jit(solution)/shard_map/ppermute | solution.py:26
  166.7 5.3 %collective-permute-start.15 = (f32[18,1,256]{2,1,0:T(1,128)S(1)}, f32[18,1,256]{2,1,0:T(1,128)S(1)}, u32[]{:S(2)}, u32[]{:S(2)}) collective-permute-start(f32[18,1,256]{2,1,0:T(1,128)S(1)} %get-tuple-element.93), channel_id=1, source_target_pairs={{4,0},{8,4},{12,8},{5,1},{9,5},{13,9},{6,2},{10,6},{14,10},{7,3},{... | collective-permute-start | bytes 55304 | tf_op jit(solution)/shard_map/ppermute | solution.py:27
  168.0 4.9 %collective-permute-start.14 = (f32[18,1,256]{2,1,0:T(1,128)S(1)}, f32[18,1,256]{2,1,0:T(1,128)S(1)}, u32[]{:S(2)}, u32[]{:S(2)}) collective-permute-start(f32[18,1,256]{2,1,0:T(1,128)S(1)} %get-tuple-element.92), channel_id=1, source_target_pairs={{0,4},{4,8},{8,12},{1,5},{5,9},{9,13},{2,6},{6,10},{10,14},{3,7},{... | collective-permute-start | bytes 55304 | tf_op jit(solution)/shard_map/ppermute | solution.py:26
  173.1 10.5 %copy-start.9 = (f32[6,22,22,3]{3,2,1,0:T(8,128)S(1)}, f32[6,22,22,3]{3,2,1,0:T(8,128)}, u32[]{:S(2)}) copy-start(f32[6,22,22,3]{3,2,1,0:T(8,128)} %copy-done.8) | copy-start | bytes 104548
  173.1 8.9 %collective-permute-start.17 = (f32[18,18,1]{2,1,0:T(8,128)S(1)}, f32[18,18,1]{2,1,0:T(8,128)S(1)}, u32[]{:S(2)}, u32[]{:S(2)}) collective-permute-start(f32[18,18,1]{2,1,0:T(8,128)S(1)} %get-tuple-element.89), channel_id=1, source_target_pairs={{1,0},{2,1},{3,2},{5,4},{6,5},{7,6},{9,8},{10,9},{11,10},{13,12},{... | collective-permute-start | bytes 3896 | tf_op jit(solution)/shard_map/ppermute | solution.py:27
  174.7 8.2 %collective-permute-start.16 = (f32[18,18,1]{2,1,0:T(8,128)S(1)}, f32[18,18,1]{2,1,0:T(8,128)S(1)}, u32[]{:S(2)}, u32[]{:S(2)}) collective-permute-start(f32[18,18,1]{2,1,0:T(8,128)S(1)} %get-tuple-element.88), channel_id=1, source_target_pairs={{0,1},{1,2},{2,3},{4,5},{5,6},{6,7},{8,9},{9,10},{10,11},{12,13},{... | collective-permute-start | bytes 3896 | tf_op jit(solution)/shard_map/ppermute | solution.py:26
  (26 other events, 152.6 us)
where the time goes:
time: 217 us; the launch traced here: 215 us
  other arithmetic  63.3 us (29%)
  Pallas kernels  55.5 us (26%)
  starting transfers between devices  52.2 us (24%)
  local copies, waits for them, and re-layouts  22 us (10%)
  waiting for transfers between devices  14.5 us (7%)
  between operations  7.48 us (3%)
    pallas_call x3, Pallas kernels, gather_rows(): pl.pallas_call(functools.partial(gather_kernel, sizes), out_shape=jax.Sha...  55.5 us
    ppermute x9, starting transfers between devices, padded(): before = lax.ppermute(last, axis, up)  35.6 us
    ppermute x9, starting transfers between devices, padded(): after = lax.ppermute(leading, axis, down)  16.6 us
    mul x7, other arithmetic, jacobi(): free_box * guess  16.5 us
    concatenate x4, other arithmetic, padded(): value = jnp.concatenate([before, value, after], axis=dim)  11.7 us
    ppermute x9, waiting for transfers between devices, padded(): after = lax.ppermute(leading, axis, down)  7.73 us
    ppermute x9, waiting for transfers between devices, padded(): before = lax.ppermute(last, axis, up)  6.79 us
    reduce_sum x2, other arithmetic, expand(): return jnp.sum(weights[:, None, None, None] * basis, axis=0)  6.5 us
  transfers between devices with their start and end apart: 18, of which 10 were waited for; matrix products, arithmetic and copies ran while one was open for 7% of the time, Pallas kernels for 9%

commit v1 on v0

--- a/solution.py
+++ b/solution.py
@@ -84,25 +84,21 @@
     return padded(field, (("gx", 0), ("gy", 1), ("gz", 2)), 2)
 
 
-def gather_kernel(sizes, row_ref, out_ref, held, local_sem, send1, recv1, send2, recv2, send3, recv3):
+def gather_kernel(sizes, row_ref, out_ref, held, local_sem, send1, recv1, send2, recv2):
     nx, ny, nz = sizes
+    plane = ny * nz
     a = lax.axis_index("gx")
     b = lax.axis_index("gy")
     c = lax.axis_index("gz")
     me = (a * ny + b) * nz + c
 
-    def along_z(k):
-        return (a, b, lax.rem(c + k, nz))
-
-    def along_y(k):
-        return (a, lax.rem(b + k, ny), c)
+    def in_plane(k):
+        return (a, lax.rem(b + k // nz, ny), lax.rem(c + k % nz, nz))
 
     def along_x(k):
         return (lax.rem(a + k, nx), b, c)
 
-    peers = [along_z(k) for k in range(1, nz)]
-    peers += [along_y(k) for k in range(1, ny)]
-    peers += [along_x(k) for k in range(1, nx)]
+    peers = [in_plane(k) for k in range(1, plane)] + [along_x(k) for k in range(1, nx)]
     barrier = pltpu.get_barrier_semaphore()
     for peer in peers:
         pl.semaphore_signal(barrier, inc=1, device_id=peer, device_id_type=MESH_ID)
@@ -134,13 +130,13 @@
                 device_id_type=MESH_ID,
             ).wait_recv()
 
-    z_first = lambda k: (a * ny + b) * nz + lax.rem(c + nz - k, nz)
-    stage(lambda k: row_ref, z_first, 1, nz, along_z, send1, recv1)
+    def p_first(k):
+        return (a * ny + lax.rem(b + ny - k // nz, ny)) * nz + lax.rem(c + nz - k % nz, nz)
+
+    stage(lambda k: row_ref, p_first, 1, plane, in_plane, send1, recv1)
     own.wait()
-    y_first = lambda k: (a * ny + lax.rem(b + ny - k, ny)) * nz
-    stage(lambda k: held.at[pl.ds(y_first(k), nz)], y_first, nz, ny, along_y, send2, recv2)
-    x_first = lambda k: lax.rem(a + nx - k, nx) * ny * nz
-    stage(lambda k: held.at[pl.ds(x_first(k), ny * nz)], x_first, ny * nz, nx, along_x, send3, recv3)
+    x_first = lambda k: lax.rem(a + nx - k, nx) * plane
+    stage(lambda k: held.at[pl.ds(x_first(k), plane)], x_first, plane, nx, along_x, send2, recv2)
     for copy in sent:
         copy.wait_send()
     final = pltpu.make_async_copy(held, out_ref, local_sem.at[1])
@@ -160,10 +156,8 @@
         scratch_shapes=[
             pltpu.VMEM((count, 1, LANES), jnp.float32),
             pltpu.SemaphoreType.DMA((2,)),
-            pltpu.SemaphoreType.DMA((sizes[2],)),
-            pltpu.SemaphoreType.DMA((sizes[2],)),
-            pltpu.SemaphoreType.DMA((sizes[1],)),
-            pltpu.SemaphoreType.DMA((sizes[1],)),
+            pltpu.SemaphoreType.DMA((sizes[1] * sizes[2],)),
+            pltpu.SemaphoreType.DMA((sizes[1] * sizes[2],)),
             pltpu.SemaphoreType.DMA((sizes[0],)),
             pltpu.SemaphoreType.DMA((sizes[0],)),
         ],

time: 217 us -> 215 us (level)
  no operation moved by 1% of the time
where the time goes in v1:
time: 215 us; the launch traced here: 213 us
  other arithmetic  63.3 us (29%)
  Pallas kernels  53.6 us (25%)
  starting transfers between devices  52.2 us (24%)
  local copies, waits for them, and re-layouts  22 us (10%)
  waiting for transfers between devices  14.5 us (7%)
  between operations  7.48 us (3%)
    pallas_call x3, Pallas kernels, gather_rows(): pl.pallas_call(functools.partial(gather_kernel, sizes), out_shape=jax.Sha...  53.6 us
    ppermute x9, starting transfers between devices, padded(): before = lax.ppermute(last, axis, up)  35.6 us
    ppermute x9, starting transfers between devices, padded(): after = lax.ppermute(leading, axis, down)  16.6 us
    mul x7, other arithmetic, jacobi(): free_box * guess  16.5 us
    concatenate x4, other arithmetic, padded(): value = jnp.concatenate([before, value, after], axis=dim)  11.7 us
    ppermute x9, waiting for transfers between devices, padded(): after = lax.ppermute(leading, axis, down)  7.73 us
    ppermute x9, waiting for transfers between devices, padded(): before = lax.ppermute(last, axis, up)  6.79 us
    reduce_sum x2, other arithmetic, expand(): return jnp.sum(weights[:, None, None, None] * basis, axis=0)  6.5 us
  transfers between devices with their start and end apart: 18, of which 10 were waited for; matrix products, arithmetic and copies ran while one was open for 7% of the time, Pallas kernels for 9%

profile of v1, /device:TPU:1, one launch (start us, length us, event | category | flops | bytes accessed | tf_op | source)
XLA Modules:
  0.0 213.5 jit_solution(7599996707249579625)
XLA Ops:
  3.3 3.3 %collective-permute-start.1 = (f32[6,3,16,256]{3,2,1,0:T(8,128)S(1)}, f32[6,3,16,256]{3,2,1,0:T(8,128)S(1)}, u32[]{:S(2)}, u32[]{:S(2)}) collective-permute-start(f32[6,3,16,256]{3,2,1,0:T(8,128)S(1)} %get-tuple-element.84), channel_id=1, source_target_pairs={{16,0},{32,16},{48,32},{64,48},{80,64},{96,80},{112,96},{17,1},{33... | collective-permute-start | bytes 884744 | tf_op jit(solution)/shard_map/ppermute | solution.py:27
  6.6 3.2 %collective-permute-start = (f32[6,3,16,256]{3,2,1,0:T(8,128)S(1)}, f32[6,3,16,256]{3,2,1,0:T(8,128)S(1)}, u32[]{:S(2)}, u32[]{:S(2)}) collective-permute-start(f32[6,3,16,256]{3,2,1,0:T(8,128)S(1)} %get-tuple-element.83), channel_id=1, source_target_pairs={{0,16},{16,32},{32,48},{48,64},{64,80},{80,96},{96,112},{1,17},{17... | collective-permute-start | bytes 884744 | tf_op jit(solution)/shard_map/ppermute | solution.py:26
  9.8 2.5 %collective-permute-done.1 = f32[6,3,16,256]{3,2,1,0:T(8,128)S(1)} collective-permute-done((f32[6,3,16,256]{3,2,1,0:T(8,128)S(1)}, f32[6,3,16,256]{3,2,1,0:T(8,128)S(1)}, u32[]{:S(2)}, u32[]{:S(2)}) %collective-permute-start.1) | collective-permute-done | bytes 294944 | tf_op jit(solution)/shard_map/ppermute | solution.py:27
  17.5 4.9 %collective-permute-start.2 = (f32[6,22,3,256]{3,1,2,0:T(8,128)}, f32[6,22,3,256]{3,1,2,0:T(8,128)}, u32[]{:S(2)}, u32[]{:S(2)}) collective-permute-start(f32[6,22,3,256]{3,1,2,0:T(8,128)} %copy.25), channel_id=1, source_target_pairs={{0,4},{4,8},{8,12},{1,5},{5,9},{9,13},{2,6},{6,10},{10,14},{3,7},{... | collective-permute-start | bytes 1216520 | tf_op jit(solution)/shard_map/ppermute | solution.py:26
  23.6 18.6 %shard_map.77 = f32[128,1,128]{2,1,0:T(1,128)} custom-call(f32[1,1,128]{2,1,0:T(1,128)} %scatter.14.row_ref), custom_call_target="tpu_custom_call" | custom-call | tf_op jit(solution)/shard_map/pallas_call | solution.py:151
  48.5 2.4 %copy.30 = f32[6,22,22,3]{2,1,3,0:T(8,128)S(1)} copy(f32[6,22,22,3]{3,2,1,0:T(8,128)} %get-tuple-element.80) | data formatting | bytes 69696 | tf_op jit(solution)/shard_map/slice | solution.py:25
  53.8 4.7 %collective-permute-start.4 = (f32[6,22,22,3]{2,1,3,0:T(8,128)}, f32[6,22,22,3]{2,1,3,0:T(8,128)}, u32[]{:S(2)}, u32[]{:S(2)}) collective-permute-start(f32[6,22,22,3]{2,1,3,0:T(8,128)} %copy.29), channel_id=1, source_target_pairs={{0,1},{1,2},{2,3},{4,5},{5,6},{6,7},{8,9},{9,10},{10,11},{12,13},{... | collective-permute-start | bytes 104552 | tf_op jit(solution)/shard_map/ppermute | solution.py:26
  58.5 3.5 %multiply_reduce_fusion.2 = f32[16,16,256]{2,1,0:T(8,128)} fusion(f32[16,16,16,256]{3,2,1,0:T(8,128)} %param.18, f32[16]{0:T(128)S(1)} %convolution_bitcast_fusion.1), kind=kLoop, calls=%fused_computation.4 | loop fusion | flops 2031616 | bytes 4456512 | tf_op jit(solution)/shard_map/reduce_sum | solution.py:77
  61.9 3.0 %copy.32 = f32[6,22,22,3]{3,2,1,0:T(8,128)} copy(f32[6,22,22,3]{2,1,3,0:T(8,128)} %collective-permute-done.5) | data formatting | bytes 69696 | tf_op jit(solution)/shard_map/ppermute | solution.py:27
  65.0 1.9 copy.31
  66.8 9.6 %pad_maximum_fusion = f32[6,22,22,262]{3,2,1,0:T(8,128)S(1)} fusion(f32[6,22,22,3]{3,2,1,0:T(8,128)} %copy.32, f32[6,22,3,256]{3,2,1,0:T(4,128)} %copy-done.20, f32[6,3,16,256]{3,2,1,0:T(8,128)} %copy-done.26, f32[1,16,16,256]{3,2,1,0:T(8,128)S(1)} %bitcast.309, f32[1,16,16,256]{3,2,1,0:T(8,128)S(1)} %fusion.198, f32[1,16,16,256]{3,2,1,0:T(8,128)S(1)} %bitcast.314, ...), kind=kLoop, calls=%fused_computation | loop fusion | flops 6847632 | bytes 6086784 | tf_op jit(solution)/shard_map/concatenate | solution.py:28
  78.1 2.4 %fusion.199 = (f32[20,20,260]{2,1,0:T(8,128)S(1)}, f32[20,20,260]{2,1,0:T(8,128)S(1)}, f32[20,20,260]{2,1,0:T(8,128)S(1)}, f32[20,20,260]{2,1,0:T(8,128)S(1)}) fusion(f32[6,22,22,262]{3,2,1,0:T(8,128)S(1)} %pad_maximum_fusion, f32[20,20,260]{2,1,0:T(8,128)S(1)} %broadcast_multiply_fusion, f32[3,20,20,260]{3,2,1,0:T(8,128)S(1)} %slice.610), kind=kLoop, calls=%fused_computation.326 | loop fusion | flops 3640000 | bytes 5824000 | tf_op jit(solution)/shard_map/mul | solution.py:67
  80.6 2.3 %fusion.205 = (f32[20,20,260]{2,1,0:T(8,128)S(1)}, f32[20,20,260]{2,1,0:T(8,128)S(1)}) fusion(f32[6,22,22,262]{3,2,1,0:T(8,128)S(1)} %pad_maximum_fusion, f32[20,20,260]{2,1,0:T(8,128)S(1)} %get-tuple-element.73, f32[20,20,260]{2,1,0:T(8,128)S(1)} %get-tuple-element.71, f32[3,20,20,260]{3,2,1,0:T(8,128)S(1)} %slice.610, f32[20,20,260]{2,1,0:T(8,128)S(1)} %get-tuple-element.72), kind=kLoop, calls=%fused_computation.344 | loop fusion | flops 3224000 | bytes 5824000 | tf_op jit(solution)/shard_map/mul | solution.py:67
  82.8 2.1 fusion.204
  87.1 2.9 %collective-permute-start.7 = (f32[3,16,256]{2,1,0:T(8,128)S(1)}, f32[3,16,256]{2,1,0:T(8,128)S(1)}, u32[]{:S(2)}, u32[]{:S(2)}) collective-permute-start(f32[3,16,256]{2,1,0:T(8,128)S(1)} %get-tuple-element.97), channel_id=1, source_target_pairs={{16,0},{32,16},{48,32},{64,48},{80,64},{96,80},{112,96},{17,1},{33... | collective-permute-start | bytes 147464 | tf_op jit(solution)/shard_map/ppermute | solution.py:27
  90.0 2.9 %collective-permute-start.6 = (f32[3,16,256]{2,1,0:T(8,128)S(1)}, f32[3,16,256]{2,1,0:T(8,128)S(1)}, u32[]{:S(2)}, u32[]{:S(2)}) collective-permute-start(f32[3,16,256]{2,1,0:T(8,128)S(1)} %get-tuple-element.96), channel_id=1, source_target_pairs={{0,16},{16,32},{32,48},{48,64},{64,80},{80,96},{96,112},{1,17},{17... | collective-permute-start | bytes 147464 | tf_op jit(solution)/shard_map/ppermute | solution.py:26
  95.8 4.6 %collective-permute-start.8 = (f32[22,3,256]{2,1,0:T(4,128)}, f32[22,3,256]{2,1,0:T(4,128)}, u32[]{:S(2)}, u32[]{:S(2)}) collective-permute-start(f32[22,3,256]{2,1,0:T(4,128)} %get-tuple-element.90), channel_id=1, source_target_pairs={{0,4},{4,8},{8,12},{1,5},{5,9},{9,13},{2,6},{6,10},{10,14},{3,7},{... | collective-permute-start | bytes 202760 | tf_op jit(solution)/shard_map/ppermute | solution.py:26
  105.0 4.0 %collective-permute-start.10 = (f32[22,22,3]{2,1,0:T(8,128)S(1)}, f32[22,22,3]{2,1,0:T(8,128)S(1)}, u32[]{:S(2)}, u32[]{:S(2)}) collective-permute-start(f32[22,22,3]{2,1,0:T(8,128)S(1)} %get-tuple-element.86), channel_id=1, source_target_pairs={{0,1},{1,2},{2,3},{4,5},{5,6},{6,7},{8,9},{9,10},{10,11},{12,13},{... | collective-permute-start | bytes 17432 | tf_op jit(solution)/shard_map/ppermute | solution.py:26
  110.5 2.8 %collective-permute-done.11 = f32[22,22,3]{2,1,0:T(8,128)S(1)} collective-permute-done((f32[22,22,3]{2,1,0:T(8,128)S(1)}, f32[22,22,3]{2,1,0:T(8,128)S(1)}, u32[]{:S(2)}, u32[]{:S(2)}) %collective-permute-start.11) | collective-permute-done | bytes 5840 | tf_op jit(solution)/shard_map/ppermute | solution.py:27
  115.7 3.0 %fusion.155 = f32[20,20,260]{2,1,0:T(8,128)S(1)} fusion(f32[22,22,262]{2,1,0:T(8,128)S(1)} %get-tuple-element.66, f32[22,22,262]{2,1,0:T(8,128)S(1)} %get-tuple-element.65, f32[6,22,22,262]{3,2,1,0:T(8,128)S(1)} %copy-done.2, f32[22,22,262]{2,1,0:T(8,128)S(1)} %get-tuple-element.75, f32[22,22,262]{2,1,0:T(8,128)S(1)} %get-tuple-element.74), kind=kLoop, calls=%fused_computation.213 | loop fusion | flops 2392000 | bytes 7072000 | tf_op jit(solution)/shard_map/add | solution.py:54
  122.1 16.6 %shard_map.78 = f32[128,1,128]{2,1,0:T(1,128)} custom-call(f32[1,1,128]{2,1,0:T(1,128)} %copy-done.37), custom_call_target="tpu_custom_call" | custom-call | tf_op jit(solution)/shard_map/pallas_call | solution.py:151
  142.4 3.6 %fusion.200 = (f32[20,20,260]{2,1,0:T(8,128)}, f32[20,20,260]{2,1,0:T(8,128)}) fusion(f32[20,20,260]{2,1,0:T(8,128)} %copy-done.6, f32[20,20,260]{2,1,0:T(8,128)} %copy-done.18, f32[6,22,22,262]{3,2,1,0:T(8,128)} %copy-done.1, f32[20,20,260]{2,1,0:T(8,128)} %copy-done.24, f32[]{:T(128)S(6)} %div.37), kind=kLoop, calls=%fused_computation.327 | loop fusion | flops 624000 | bytes 2912004 | tf_op jit(solution)/shard_map/mul | solution.py:67
  146.4 3.0 %multiply_reduce_fusion = f32[16,16,256]{2,1,0:T(8,128)S(1)} fusion(f32[16,16,16,256]{3,2,1,0:T(8,128)} %param.18, f32[16]{0:T(128)S(1)} %convolution_bitcast_fusion), kind=kLoop, calls=%fused_computation.2 | loop fusion | flops 2031616 | bytes 4456512 | tf_op jit(solution)/shard_map/reduce_sum | solution.py:77
  149.5 4.0 %fusion.203 = (f32[20,20,260]{2,1,0:T(8,128)S(1)}, f32[20,20,260]{2,1,0:T(8,128)S(1)}) fusion(f32[6,22,22,262]{3,2,1,0:T(8,128)} %copy-done.1, f32[20,20,260]{2,1,0:T(8,128)S(1)} %copy-done.7, f32[20,20,260]{2,1,0:T(8,128)S(1)} %copy-done.17, f32[20,20,260]{2,1,0:T(8,128)S(1)} %copy-done.30, f32[3,20,20,260]{3,2,1,0:T(8,128)S(1)} %slice.610, ...), kind=kLoop, calls=%fused_computation.342 | loop fusion | flops 3224000 | bytes 5824000 | tf_op jit(solution)/shard_map/mul | solution.py:67
  158.8 2.3 %collective-permute-start.13 = (f32[1,16,256]{2,1,0:T(8,128)S(1)}, f32[1,16,256]{2,1,0:T(8,128)S(1)}, u32[]{:S(2)}, u32[]{:S(2)}) collective-permute-start(f32[1,16,256]{2,1,0:T(8,128)S(1)} %get-tuple-element.95), channel_id=1, source_target_pairs={{16,0},{32,16},{48,32},{64,48},{80,64},{96,80},{112,96},{17,1},{33... | collective-permute-start | bytes 49160 | tf_op jit(solution)/shard_map/ppermute | solution.py:27
  161.1 3.3 %collective-permute-start.12 = (f32[1,16,256]{2,1,0:T(8,128)S(1)}, f32[1,16,256]{2,1,0:T(8,128)S(1)}, u32[]{:S(2)}, u32[]{:S(2)}) collective-permute-start(f32[1,16,256]{2,1,0:T(8,128)S(1)} %get-tuple-element.94), channel_id=1, source_target_pairs={{0,16},{16,32},{32,48},{48,64},{64,80},{80,96},{96,112},{1,17},{17... | collective-permute-start | bytes 49160 | tf_op jit(solution)/shard_map/ppermute | solution.py:26
  166.5 4.0 %collective-permute-start.14 = (f32[18,1,256]{2,1,0:T(1,128)S(1)}, f32[18,1,256]{2,1,0:T(1,128)S(1)}, u32[]{:S(2)}, u32[]{:S(2)}) collective-permute-start(f32[18,1,256]{2,1,0:T(1,128)S(1)} %get-tuple-element.92), channel_id=1, source_target_pairs={{0,4},{4,8},{8,12},{1,5},{5,9},{9,13},{2,6},{6,10},{10,14},{3,7},{... | collective-permute-start | bytes 55304 | tf_op jit(solution)/shard_map/ppermute | solution.py:26
  173.3 4.0 %collective-permute-start.16 = (f32[18,18,1]{2,1,0:T(8,128)S(1)}, f32[18,18,1]{2,1,0:T(8,128)S(1)}, u32[]{:S(2)}, u32[]{:S(2)}) collective-permute-start(f32[18,18,1]{2,1,0:T(8,128)S(1)} %get-tuple-element.88), channel_id=1, source_target_pairs={{0,1},{1,2},{2,3},{4,5},{5,6},{6,7},{8,9},{9,10},{10,11},{12,13},{... | collective-permute-start | bytes 3896 | tf_op jit(solution)/shard_map/ppermute | solution.py:26
  178.1 2.5 %collective-permute-done.17 = f32[18,18,1]{2,1,0:T(8,128)S(1)} collective-permute-done((f32[18,18,1]{2,1,0:T(8,128)S(1)}, f32[18,18,1]{2,1,0:T(8,128)S(1)}, u32[]{:S(2)}, u32[]{:S(2)}) %collective-permute-start.17) | collective-permute-done | bytes 1328 | tf_op jit(solution)/shard_map/ppermute | solution.py:27
  183.7 2.7 %maximum_bitcast_fusion.1 = f32[1,1,4]{2,1,0:T(1,128)S(1)} fusion(f32[1]{0:T(128)} %bitcast.39, f32[1]{0:T(128)} %bitcast.38, f32[1]{0:T(128)} %bitcast.37, f32[1]{0:T(128)} %bitcast.29), kind=kLoop, calls=%fused_computation.338 | loop fusion | flops 12 | bytes 32 | tf_op jit(solution)/shard_map/broadcast_in_dim;broadcast_in_dim | solution.py:150
  186.9 18.4 %shard_map.79 = f32[128,1,128]{2,1,0:T(1,128)} custom-call(f32[1,1,128]{2,1,0:T(1,128)} %scatter.19.row_ref), custom_call_target="tpu_custom_call" | custom-call | tf_op jit(solution)/shard_map/pallas_call | solution.py:151
  211.4 2.1 multiply_subtract_fusion.1
  (152 shorter events, 55.2 us)
Async XLA Ops:
  0.6 42.5 %copy-start = (f32[16,2048]{1,0:T(8,128)S(1)}, f32[16,2048]{1,0:T(8,128)}, u32[]{:S(2)}) copy-start(f32[16,2048]{1,0:T(8,128)} %param.19) | copy-start | bytes 393220
  0.6 21.8 %copy-start.10 = (f32[16,16,256]{2,1,0:T(8,128)S(1)}, f32[16,16,256]{2,1,0:T(8,128)}, u32[]{:S(2)}) copy-start(f32[16,16,256]{2,1,0:T(8,128)} %param.14) | copy-start | bytes 786436
  0.7 21.8 %copy-start.3 = (f32[16,16,16,256]{3,2,1,0:T(8,128)S(1)}, f32[16,16,16,256]{3,2,1,0:T(8,128)}, u32[]{:S(2)}) copy-start(f32[16,16,16,256]{3,2,1,0:T(8,128)} %param.18) | copy-start | bytes 12582916
  1.8 65.0 %copy-start.13 = (f32[1,16,16,256]{3,2,1,0:T(8,128)}, f32[1,16,16,256]{3,2,1,0:T(8,128)S(1)}, u32[]{:S(2)}) copy-start(f32[1,16,16,256]{3,2,1,0:T(8,128)S(1)} %fusion.198) | copy-start | bytes 786436
  3.3 9.0 %collective-permute-start.1 = (f32[6,3,16,256]{3,2,1,0:T(8,128)S(1)}, f32[6,3,16,256]{3,2,1,0:T(8,128)S(1)}, u32[]{:S(2)}, u32[]{:S(2)}) collective-permute-start(f32[6,3,16,256]{3,2,1,0:T(8,128)S(1)} %get-tuple-element.84), channel_id=1, source_target_pairs={{16,0},{32,16},{48,32},{64,48},{80,64},{96,80},{112,96},{17,1},{33... | collective-permute-start | bytes 884744 | tf_op jit(solution)/shard_map/ppermute | solution.py:27
  6.6 6.8 %collective-permute-start = (f32[6,3,16,256]{3,2,1,0:T(8,128)S(1)}, f32[6,3,16,256]{3,2,1,0:T(8,128)S(1)}, u32[]{:S(2)}, u32[]{:S(2)}) collective-permute-start(f32[6,3,16,256]{3,2,1,0:T(8,128)S(1)} %get-tuple-element.83), channel_id=1, source_target_pairs={{0,16},{16,32},{32,48},{48,64},{64,80},{80,96},{96,112},{1,17},{17... | collective-permute-start | bytes 884744 | tf_op jit(solution)/shard_map/ppermute | solution.py:26
  12.3 32.7 %copy-start.26 = (f32[6,3,16,256]{3,2,1,0:T(8,128)}, f32[6,3,16,256]{3,2,1,0:T(8,128)S(1)}, u32[]{:S(2)}) copy-start(f32[6,3,16,256]{3,2,1,0:T(8,128)S(1)} %collective-permute-done.1) | copy-start | bytes 884740
  13.5 31.6 %copy-start.28 = (f32[6,3,16,256]{3,2,1,0:T(8,128)}, f32[6,3,16,256]{3,2,1,0:T(8,128)S(1)}, u32[]{:S(2)}) copy-start(f32[6,3,16,256]{3,2,1,0:T(8,128)S(1)} %collective-permute-done) | copy-start | bytes 884740
  15.2 30.8 %copy-start.5 = (f32[3,16,16,256]{3,2,1,0:T(8,128)S(1)}, f32[3,16,16,256]{3,2,1,0:T(8,128)}, u32[]{:S(2)}) copy-start(f32[3,16,16,256]{3,2,1,0:T(8,128)} %param.15) | copy-start | bytes 2359300
  15.2 30.8 %copy-start.15 = (f32[16,16,256]{2,1,0:T(8,128)S(1)}, f32[16,16,256]{2,1,0:T(8,128)}, u32[]{:S(2)}) copy-start(f32[16,16,256]{2,1,0:T(8,128)} %param.16) | copy-start | bytes 786436
  15.3 28.0 %collective-permute-start.3 = (f32[6,22,3,256]{3,1,2,0:T(8,128)S(1)}, f32[6,22,3,256]{3,1,2,0:T(8,128)S(1)}, u32[]{:S(2)}, u32[]{:S(2)}) collective-permute-start(f32[6,22,3,256]{3,1,2,0:T(8,128)S(1)} %copy.26), channel_id=1, source_target_pairs={{4,0},{8,4},{12,8},{5,1},{9,5},{13,9},{6,2},{10,6},{14,10},{7,3},{... | collective-permute-start | bytes 1216520 | tf_op jit(solution)/shard_map/ppermute | solution.py:27
  17.5 26.1 %collective-permute-start.2 = (f32[6,22,3,256]{3,1,2,0:T(8,128)}, f32[6,22,3,256]{3,1,2,0:T(8,128)}, u32[]{:S(2)}, u32[]{:S(2)}) collective-permute-start(f32[6,22,3,256]{3,1,2,0:T(8,128)} %copy.25), channel_id=1, source_target_pairs={{0,4},{4,8},{8,12},{1,5},{5,9},{9,13},{2,6},{6,10},{10,14},{3,7},{... | collective-permute-start | bytes 1216520 | tf_op jit(solution)/shard_map/ppermute | solution.py:26
  50.8 11.1 %collective-permute-start.5 = (f32[6,22,22,3]{2,1,3,0:T(8,128)S(1)}, f32[6,22,22,3]{2,1,3,0:T(8,128)}, u32[]{:S(2)}, u32[]{:S(2)}) collective-permute-start(f32[6,22,22,3]{2,1,3,0:T(8,128)S(1)} %copy.30), channel_id=1, source_target_pairs={{1,0},{2,1},{3,2},{5,4},{6,5},{7,6},{9,8},{10,9},{11,10},{13,12},{... | collective-permute-start | bytes 104552 | tf_op jit(solution)/shard_map/ppermute | solution.py:27
  53.8 11.2 %collective-permute-start.4 = (f32[6,22,22,3]{2,1,3,0:T(8,128)}, f32[6,22,22,3]{2,1,3,0:T(8,128)}, u32[]{:S(2)}, u32[]{:S(2)}) collective-permute-start(f32[6,22,22,3]{2,1,3,0:T(8,128)} %copy.29), channel_id=1, source_target_pairs={{0,1},{1,2},{2,3},{4,5},{5,6},{6,7},{8,9},{9,10},{10,11},{12,13},{... | collective-permute-start | bytes 104552 | tf_op jit(solution)/shard_map/ppermute | solution.py:26
  84.9 15.5 %copy-start.35 = (f32[128,1,128]{2,1,0:T(1,128)S(1)}, f32[128,1,128]{2,1,0:T(1,128)}, u32[]{:S(2)}) copy-start(f32[128,1,128]{2,1,0:T(1,128)} %shard_map.77) | copy-start | bytes 196612
  87.1 5.8 %collective-permute-start.7 = (f32[3,16,256]{2,1,0:T(8,128)S(1)}, f32[3,16,256]{2,1,0:T(8,128)S(1)}, u32[]{:S(2)}, u32[]{:S(2)}) collective-permute-start(f32[3,16,256]{2,1,0:T(8,128)S(1)} %get-tuple-element.97), channel_id=1, source_target_pairs={{16,0},{32,16},{48,32},{64,48},{80,64},{96,80},{112,96},{17,1},{33... | collective-permute-start | bytes 147464 | tf_op jit(solution)/shard_map/ppermute | solution.py:27
  90.0 3.9 %collective-permute-start.6 = (f32[3,16,256]{2,1,0:T(8,128)S(1)}, f32[3,16,256]{2,1,0:T(8,128)S(1)}, u32[]{:S(2)}, u32[]{:S(2)}) collective-permute-start(f32[3,16,256]{2,1,0:T(8,128)S(1)} %get-tuple-element.96), channel_id=1, source_target_pairs={{0,16},{16,32},{32,48},{48,64},{64,80},{80,96},{96,112},{1,17},{17... | collective-permute-start | bytes 147464 | tf_op jit(solution)/shard_map/ppermute | solution.py:26
  94.5 6.6 %collective-permute-start.9 = (f32[22,3,256]{2,1,0:T(4,128)}, f32[22,3,256]{2,1,0:T(4,128)}, u32[]{:S(2)}, u32[]{:S(2)}) collective-permute-start(f32[22,3,256]{2,1,0:T(4,128)} %get-tuple-element.91), channel_id=1, source_target_pairs={{4,0},{8,4},{12,8},{5,1},{9,5},{13,9},{6,2},{10,6},{14,10},{7,3},{... | collective-permute-start | bytes 202760 | tf_op jit(solution)/shard_map/ppermute | solution.py:27
  95.8 6.6 %collective-permute-start.8 = (f32[22,3,256]{2,1,0:T(4,128)}, f32[22,3,256]{2,1,0:T(4,128)}, u32[]{:S(2)}, u32[]{:S(2)}) collective-permute-start(f32[22,3,256]{2,1,0:T(4,128)} %get-tuple-element.90), channel_id=1, source_target_pairs={{0,4},{4,8},{8,12},{1,5},{5,9},{9,13},{2,6},{6,10},{10,14},{3,7},{... | collective-permute-start | bytes 202760 | tf_op jit(solution)/shard_map/ppermute | solution.py:26
  101.1 13.1 %copy-start.2 = (f32[6,22,22,262]{3,2,1,0:T(8,128)S(1)}, f32[6,22,22,262]{3,2,1,0:T(8,128)}, u32[]{:S(2)}) copy-start(f32[6,22,22,262]{3,2,1,0:T(8,128)} %copy-done.1) | copy-start | bytes 9130180
  103.7 9.6 %collective-permute-start.11 = (f32[22,22,3]{2,1,0:T(8,128)S(1)}, f32[22,22,3]{2,1,0:T(8,128)S(1)}, u32[]{:S(2)}, u32[]{:S(2)}) collective-permute-start(f32[22,22,3]{2,1,0:T(8,128)S(1)} %get-tuple-element.87), channel_id=1, source_target_pairs={{1,0},{2,1},{3,2},{5,4},{6,5},{7,6},{9,8},{10,9},{11,10},{13,12},{... | collective-permute-start | bytes 17432 | tf_op jit(solution)/shard_map/ppermute | solution.py:27
  105.0 9.2 %collective-permute-start.10 = (f32[22,22,3]{2,1,0:T(8,128)S(1)}, f32[22,22,3]{2,1,0:T(8,128)S(1)}, u32[]{:S(2)}, u32[]{:S(2)}) collective-permute-start(f32[22,22,3]{2,1,0:T(8,128)S(1)} %get-tuple-element.86), channel_id=1, source_target_pairs={{0,1},{1,2},{2,3},{4,5},{5,6},{6,7},{8,9},{9,10},{10,11},{12,13},{... | collective-permute-start | bytes 17432 | tf_op jit(solution)/shard_map/ppermute | solution.py:26
  119.5 26.6 %copy-start.36 = (f32[2048]{0:T(1024)S(1)}, f32[2048]{0:T(1024)}, u32[]{:S(2)}) copy-start(f32[2048]{0:T(1024)} %reshape.101) | copy-start | bytes 24580
  155.4 21.9 %copy-start.14 = (f32[1,16,16,256]{3,2,1,0:T(8,128)S(1)}, f32[1,16,16,256]{3,2,1,0:T(8,128)}, u32[]{:S(2)}) copy-start(f32[1,16,16,256]{3,2,1,0:T(8,128)} %copy-done.13) | copy-start | bytes 786436
  155.4 21.9 %copy-start.16 = (f32[16,16,256]{2,1,0:T(8,128)S(1)}, f32[16,16,256]{2,1,0:T(8,128)}, u32[]{:S(2)}) copy-start(f32[16,16,256]{2,1,0:T(8,128)} %param.16) | copy-start | bytes 786436
  158.8 5.6 %collective-permute-start.13 = (f32[1,16,256]{2,1,0:T(8,128)S(1)}, f32[1,16,256]{2,1,0:T(8,128)S(1)}, u32[]{:S(2)}, u32[]{:S(2)}) collective-permute-start(f32[1,16,256]{2,1,0:T(8,128)S(1)} %get-tuple-element.95), channel_id=1, source_target_pairs={{16,0},{32,16},{48,32},{64,48},{80,64},{96,80},{112,96},{17,1},{33... | collective-permute-start | bytes 49160 | tf_op jit(solution)/shard_map/ppermute | solution.py:27
  161.1 4.1 %collective-permute-start.12 = (f32[1,16,256]{2,1,0:T(8,128)S(1)}, f32[1,16,256]{2,1,0:T(8,128)S(1)}, u32[]{:S(2)}, u32[]{:S(2)}) collective-permute-start(f32[1,16,256]{2,1,0:T(8,128)S(1)} %get-tuple-element.94), channel_id=1, source_target_pairs={{0,16},{16,32},{32,48},{48,64},{64,80},{80,96},{96,112},{1,17},{17... | collective-permute-start | bytes 49160 | tf_op jit(solution)/shard_map/ppermute | solution.py:26
  165.2 5.3 %collective-permute-start.15 = (f32[18,1,256]{2,1,0:T(1,128)S(1)}, f32[18,1,256]{2,1,0:T(1,128)S(1)}, u32[]{:S(2)}, u32[]{:S(2)}) collective-permute-start(f32[18,1,256]{2,1,0:T(1,128)S(1)} %get-tuple-element.93), channel_id=1, source_target_pairs={{4,0},{8,4},{12,8},{5,1},{9,5},{13,9},{6,2},{10,6},{14,10},{7,3},{... | collective-permute-start | bytes 55304 | tf_op jit(solution)/shard_map/ppermute | solution.py:27
  166.5 4.9 %collective-permute-start.14 = (f32[18,1,256]{2,1,0:T(1,128)S(1)}, f32[18,1,256]{2,1,0:T(1,128)S(1)}, u32[]{:S(2)}, u32[]{:S(2)}) collective-permute-start(f32[18,1,256]{2,1,0:T(1,128)S(1)} %get-tuple-element.92), channel_id=1, source_target_pairs={{0,4},{4,8},{8,12},{1,5},{5,9},{9,13},{2,6},{6,10},{10,14},{3,7},{... | collective-permute-start | bytes 55304 | tf_op jit(solution)/shard_map/ppermute | solution.py:26
  171.6 10.5 %copy-start.9 = (f32[6,22,22,3]{3,2,1,0:T(8,128)S(1)}, f32[6,22,22,3]{3,2,1,0:T(8,128)}, u32[]{:S(2)}) copy-start(f32[6,22,22,3]{3,2,1,0:T(8,128)} %copy-done.8) | copy-start | bytes 104548
  171.7 8.9 %collective-permute-start.17 = (f32[18,18,1]{2,1,0:T(8,128)S(1)}, f32[18,18,1]{2,1,0:T(8,128)S(1)}, u32[]{:S(2)}, u32[]{:S(2)}) collective-permute-start(f32[18,18,1]{2,1,0:T(8,128)S(1)} %get-tuple-element.89), channel_id=1, source_target_pairs={{1,0},{2,1},{3,2},{5,4},{6,5},{7,6},{9,8},{10,9},{11,10},{13,12},{... | collective-permute-start | bytes 3896 | tf_op jit(solution)/shard_map/ppermute | solution.py:27
  173.3 8.2 %collective-permute-start.16 = (f32[18,18,1]{2,1,0:T(8,128)S(1)}, f32[18,18,1]{2,1,0:T(8,128)S(1)}, u32[]{:S(2)}, u32[]{:S(2)}) collective-permute-start(f32[18,18,1]{2,1,0:T(8,128)S(1)} %get-tuple-element.88), channel_id=1, source_target_pairs={{0,1},{1,2},{2,3},{4,5},{5,6},{6,7},{8,9},{9,10},{10,11},{12,13},{... | collective-permute-start | bytes 3896 | tf_op jit(solution)/shard_map/ppermute | solution.py:26
  (26 other events, 152.6 us)
